TPU v7x, 256 devices: a whole 4x4x8 slice. The times are simulated.
256 devices in a mesh: outer: 8 (over z), inner: 32 (over y, x, core).
Axes of the slice: x: 4, y: 4, z: 8, core: 2. Of those that a mesh axis runs over, the one named last changes fastest.
Arguments:
- context: bfloat16 [32768, 4096], P(('outer', 'inner')), may hold values from -5 to 5
- query_acts: bfloat16 [64, 4096], replicated, may hold values from -5 to 5
- norm_gain: float32 [4096], replicated, may hold values from 0.25 to 1.75
- w_query: bfloat16 [4096, 2048], P('inner'), may hold values from -0.078125 to 0.078125
- w_key: bfloat16 [4096, 512], P('inner'), may hold values from -0.453125 to 0.453125
- value_weight: bfloat16 [4096, 512], P('inner'), may hold values from -0.09375 to 0.09375
- lengths: int32 [256], replicated, may hold values from 64 to 128, as said below
Outputs:
- block_out: bfloat16 [32768, 2048], P(('outer', 'inner'))
- query_out: bfloat16 [64, 2048], replicated
Inputs may be any that keep to these rules, and one draw needn't show every extreme that they name: `lengths`: valid tokens of a block are its first ones; the rest of it is padding.
All inputs are finite; a program needn't handle non-finite values.
Results may differ from a plain program's by a relative error of at most 0.004.
The roundings to bfloat16 on the way count: a program that leaves them out, or rounds other values in their place, can miss the bound.
Values may be sent and summed in bfloat16 or wider, within the bound.
No kernel may reach another device: no remote copies, remote signals or barrier semaphores. Data moves between devices by JAX's collectives and lax.ppermute only.
A program may use at most 320 MiB of HBM per device.

v0:
```python
import jax
import jax.numpy as jnp
from jax import lax
from jax.sharding import PartitionSpec as P

QUERY_HEADS = 16
KEY_VALUE_HEADS = 4
HEAD_SIZE = 128
epsilon = 1e-05


def broadcast(block, axis, owner):
    block = jnp.where(lax.axis_index(axis) == owner, block, jnp.zeros_like(block))
    return lax.psum(block, axis)


def normalize(matrix, norm_gain):
    widened = matrix.astype(jnp.float32)
    factor = lax.rsqrt(jnp.mean(widened * widened, axis=-1, keepdims=True) + epsilon)
    return (widened * factor * norm_gain).astype(jnp.bfloat16)


def attend_part(query_rows, key_row_block, value_matrix, allowed):
    count_of_rows = query_rows.shape[0]
    head_groups = query_rows.reshape(
        count_of_rows, KEY_VALUE_HEADS, QUERY_HEADS // KEY_VALUE_HEADS, HEAD_SIZE
    )
    per_head_keys = key_row_block.reshape(key_row_block.shape[0], KEY_VALUE_HEADS, HEAD_SIZE)
    per_head_values = value_matrix.reshape(value_matrix.shape[0], KEY_VALUE_HEADS, HEAD_SIZE)
    scores = jnp.einsum(
        "rhgd,khd->hgrk", head_groups, per_head_keys, preferred_element_type=jnp.float32
    ) * HEAD_SIZE ** (-0.5)
    scores = jnp.where(allowed, scores, -jnp.inf)
    maxima = jnp.max(scores, axis=-1)
    weights = jnp.exp(scores - maxima[..., None])
    sum_exp = jnp.sum(weights, axis=-1)
    numerator = jnp.einsum(
        "hgrk,khd->rhgd",
        weights.astype(jnp.bfloat16),
        per_head_values,
        preferred_element_type=jnp.float32,
    )
    return (
        maxima.reshape(QUERY_HEADS, count_of_rows),
        sum_exp.reshape(QUERY_HEADS, count_of_rows),
        numerator.reshape(count_of_rows, QUERY_HEADS * HEAD_SIZE),
    )


def spread(factor):
    return jnp.repeat(factor.T, HEAD_SIZE, axis=1)


def combine(former, latter):
    maxima = jnp.maximum(former[0], latter[0])
    scale_one = jnp.exp(former[0] - maxima)
    scale_two = jnp.exp(latter[0] - maxima)
    return (
        maxima,
        former[1] * scale_one + latter[1] * scale_two,
        former[2] * spread(scale_one) + latter[2] * spread(scale_two),
    )


def finish(pieces):
    return (pieces[2] / spread(pieces[1])).astype(jnp.bfloat16)


def share_anchor(stacked):
    return broadcast(stacked, ("outer", "inner"), 0)


def per_device(context, query_acts, norm_gain, w_query, w_key, value_weight, lengths):
    block_rows = context.shape[0]
    normed = jnp.concatenate(
        [normalize(context, norm_gain), normalize(query_acts, norm_gain)], axis=0
    )

    def apply_weight(whole_weight):
        return jnp.dot(normed, whole_weight, preferred_element_type=jnp.float32).astype(
            jnp.bfloat16
        )

    whole_q, whole_k, whole_v = (
        lax.all_gather(w_query, "inner", axis=0, tiled=True),
        lax.all_gather(w_key, "inner", axis=0, tiled=True),
        lax.all_gather(value_weight, "inner", axis=0, tiled=True),
    )
    projected_k = apply_weight(whole_k)
    projected_v = apply_weight(whole_v)
    anchor = share_anchor(jnp.stack([projected_k[:block_rows], projected_v[:block_rows]]))
    projected_q = apply_weight(whole_q)
    position = lax.axis_index(("outer", "inner"))
    own_length = lengths[position]
    anchor_length = lengths[0]
    places = jnp.arange(block_rows, dtype=jnp.int32)
    causal = places[:, None] >= places[None, :]
    block_q = projected_q[:block_rows]
    block_k = projected_k[:block_rows]
    block_v = projected_v[:block_rows]
    query_q = projected_q[block_rows:]
    query_k = projected_k[block_rows:]
    query_v = projected_v[block_rows:]
    query_count = query_q.shape[0]
    own_allowed = causal & (places[None, :] < own_length)
    anchor_allowed = jnp.broadcast_to(
        (places[None, :] < anchor_length) & (position > 0), (block_rows, block_rows)
    )
    allowed = jnp.concatenate([anchor_allowed, own_allowed], axis=1)
    key_row_block = jnp.concatenate([anchor[0], block_k], axis=0)
    value_rows = jnp.concatenate([anchor[1], block_v], axis=0)
    block_out = finish(attend_part(block_q, key_row_block, value_rows, allowed))
    reached = jnp.broadcast_to(places[None, :] < own_length, (query_count, block_rows))
    block_part = attend_part(query_q, block_k, block_v, reached)
    highest = lax.pmax(block_part[0], ("outer", "inner"))
    rescale = jnp.exp(block_part[0] - highest)
    summed_parts = lax.psum(
        (block_part[1] * rescale, block_part[2] * spread(rescale)), ("outer", "inner")
    )
    merged = (highest, summed_parts[0], summed_parts[1])
    query_places = jnp.arange(query_count, dtype=jnp.int32)
    self_part = attend_part(
        query_q, query_k, query_v, query_places[:, None] >= query_places[None, :]
    )
    return (block_out, finish(combine(merged, self_part)))


def solution(mesh):
    in_specs = (
        P(("outer", "inner"), None),
        P(),
        P(),
        P("inner", None),
        P("inner", None),
        P("inner", None),
        P(),
    )
    out_specs = (P(("outer", "inner"), None), P())
    return jax.shard_map(
        per_device, mesh=mesh, in_specs=in_specs, out_specs=out_specs, check_vma=False
    )
```

profile of v0, /device:TPU:2, one launch (start us, length us, event | category | flops | bytes accessed | tf_op | source)
XLA Modules:
  0.0 875.9 jit_solution(4082930749184454192)
XLA Ops:
  7.2 0.7 all-gather.4.cloned.1.call-update
  8.0 0.7 all-gather.6.cloned.1.call-update
  8.7 0.0 all-reduce.3.cloned.1.call-start
  8.7 1.2 fusion.9
  10.0 1.5 fusion
  11.5 0.9 fusion.11
  12.5 0.3 fusion.2
  12.8 51.5 %all-gather.4.cloned.1.call-done = bf16[4096,512]{1,0:T(8,128)(2,1)} async-done(((bf16[128,512]{1,0:T(8,128)(2,1)}), bf16[4096,512]{1,0:T(8,128)(2,1)}) %all-gather.4.cloned.1.call-update) | async-done | bytes 4194320 | tf_op jit(solution)/shard_map/all_gather | solution.py:86
  64.3 3.2 convolution_convert_fusion.2
  67.6 49.9 %all-gather.6.cloned.1.call-done = bf16[4096,512]{1,0:T(8,128)(2,1)} async-done(((bf16[128,512]{1,0:T(8,128)(2,1)}), bf16[4096,512]{1,0:T(8,128)(2,1)}) %all-gather.6.cloned.1.call-update) | async-done | bytes 4194320 | tf_op jit(solution)/shard_map/all_gather | solution.py:87
  117.5 3.2 convolution_convert_fusion.1
  120.7 0.7 maximum_select_fusion
  121.4 0.0 all-gather.8.cloned.1.call-start
  121.5 0.5 all-gather.8.cloned.1.call-update
  122.0 0.0 all-reduce.5.cloned.1.call-start
  122.1 0.6 fusion.52
  122.7 0.6 compare_and_fusion
  123.2 0.6 iota_compare_fusion.2
  123.8 0.1 fusion.37
  123.9 0.1 pad_add_fusion
  124.1 0.8 copy.28
  124.9 0.7 concatenate.28
  125.6 0.6 reshape.106
  126.2 0.6 reshape.109
  126.9 246.7 %all-reduce.3.cloned.1.call-done = bf16[2,128,512]{2,1,0:T(8,128)(2,1)} async-done(((bf16[2,128,512]{2,1,0:T(8,128)(2,1)}), bf16[2,128,512]{2,1,0:T(8,128)(2,1)}) %all-reduce.3.cloned.1.call-update) | async-done | bytes 262160 | tf_op jit(solution)/shard_map/psum | solution.py:14
  373.5 1.0 fusion.49
  374.6 0.8 copy.56
  375.4 76.8 %all-gather.8.cloned.1.call-done = bf16[4096,2048]{1,0:T(8,128)(2,1)} async-done(((bf16[128,2048]{1,0:T(8,128)(2,1)}), bf16[4096,2048]{1,0:T(8,128)(2,1)}) %all-gather.8.cloned.1.call-update) | async-done | bytes 16777232 | tf_op jit(solution)/shard_map/all_gather | solution.py:85
  452.2 7.7 convolution_convert_fusion
  459.9 0.4 reshape.98
  460.3 0.5 fusion.53
  460.8 0.3 fusion.3
  461.1 0.1 copy-done.5
  461.2 0.1 copy-done.6
  461.2 0.5 fusion.12
  461.8 0.3 copy.34
  462.1 0.1 copy.33
  462.2 0.2 reshape.102
  462.4 0.3 copy-done.9
  462.7 0.4 fusion.54
  463.1 76.0 %pmax.7 = f32[16,64]{1,0:T(8,128)S(1)} all-reduce(f32[16,64]{1,0:T(8,128)S(1)} %bitcast.97), channel_id=1, replica_groups=mesh['outer'=8,'inner'=32] {'outer','inner'}, use_global_device_ids=true, to_apply=%region_6.7 | all-reduce | flops 1024 | bytes 8192 | tf_op jit(solution)/shard_map/pmax | solution.py:115
  539.1 0.4 fusion.19
  539.5 74.4 %psum.23 = f32[16,64]{1,0:T(8,128)S(1)} all-reduce(f32[16,64]{1,0:T(8,128)S(1)} %get-tuple-element.13), channel_id=1, replica_groups=mesh['outer'=8,'inner'=32] {'outer','inner'}, use_global_device_ids=true, to_apply=%region_10.11 | all-reduce | flops 1024 | bytes 8192 | tf_op jit(solution)/shard_map/psum | solution.py:117
  614.0 0.4 fusion.55
  614.4 0.1 fusion.21
  614.5 0.1 copy.47
  614.6 0.3 convolution_bitcast_fusion
  614.9 0.3 copy.45
  615.2 0.2 reshape.110
  615.4 0.1 copy.46
  615.5 0.3 convolution_bitcast_fusion.1
  615.8 0.3 copy.38
  616.2 0.2 reshape.103
  616.4 0.1 copy.39
  616.5 0.2 broadcast_in_dim.71
  616.7 1.0 bitcast_multiply_fusion.2
  617.7 0.1 copy.42
  617.8 0.3 broadcast_in_dim.68
  618.2 1.2 fusion.14
  619.3 247.2 %all-reduce.5.cloned.1.call-done = f32[64,2048]{1,0:T(8,128)} async-done(((f32[64,2048]{1,0:T(8,128)}), f32[64,2048]{1,0:T(8,128)}) %all-reduce.5.cloned.1.call-update) | async-done | bytes 524304 | tf_op jit(solution)/shard_map/psum | solution.py:117
  866.5 0.2 broadcast_in_dim.76
  866.7 0.2 broadcast_in_dim.75
  866.9 0.2 broadcast_in_dim.74
  867.1 2.2 fusion.16
  (42 shorter events, 0.4 us)
Async XLA Ops:
  7.2 4.4 copy-start.1
  7.2 5.3 copy-start
  7.2 5.3 copy-start.10
  7.2 57.1 %all-gather.4.cloned.1.call-start = ((), (), s32[]{:S(2)}) async-start(), calls=%async_computation | async-start | bytes 4325376 | tf_op jit(solution)/shard_map/all_gather | solution.py:86
  7.9 109.5 %all-gather.6.cloned.1.call-start = ((), (), s32[]{:S(2)}) async-start(), calls=%async_computation.1 | async-start | bytes 4325376 | tf_op jit(solution)/shard_map/all_gather | solution.py:87
  8.7 364.9 %all-reduce.3.cloned.1.call-start = ((), (), s32[]{:S(2)}) async-start(), calls=%async_computation.2 | async-start | bytes 524288 | tf_op jit(solution)/shard_map/psum | solution.py:14
  12.5 105.0 %copy-start.3 = (bf16[64,4096]{1,0:T(8,128)(2,1)}, bf16[64,4096]{1,0:T(8,128)(2,1)S(1)}, u32[]{:S(2)}) copy-start(bf16[64,4096]{1,0:T(8,128)(2,1)S(1)} %fusion.11) | copy-start | bytes 1572868
  67.6 54.5 %copy-start.11 = (s32[256]{0:T(256)S(1)}, s32[256]{0:T(256)}, u32[]{:S(2)}) copy-start(s32[256]{0:T(256)} %param.13) | copy-start | bytes 3076
  120.6 331.5 %copy-start.4 = (bf16[64,4096]{1,0:T(8,128)(2,1)S(1)}, bf16[64,4096]{1,0:T(8,128)(2,1)}, u32[]{:S(2)}) copy-start(bf16[64,4096]{1,0:T(8,128)(2,1)} %copy-done.3) | copy-start | bytes 1572868
  121.4 330.7 %all-gather.8.cloned.1.call-start = ((), (), s32[]{:S(2)}) async-start(), calls=%async_computation.3 | async-start | bytes 17301504 | tf_op jit(solution)/shard_map/all_gather | solution.py:85
  122.0 744.5 %all-reduce.5.cloned.1.call-start = ((), (), s32[]{:S(2)}) async-start(), calls=%async_computation.4 | async-start | bytes 1048576 | tf_op jit(solution)/shard_map/psum | solution.py:117
  459.8 0.9 copy-start.2
  460.3 0.9 copy-start.5
  460.3 1.0 copy-start.6
  461.2 1.0 slice-start
  461.7 0.9 copy-start.9
  461.8 152.2 %copy-start.8 = (bf16[64,4,128]{2,1,0:T(4,128)(2,1)S(1)}, bf16[64,4,128]{2,1,0:T(4,128)(2,1)}, u32[]{:S(2)}) copy-start(bf16[64,4,128]{2,1,0:T(4,128)(2,1)} %reshape.106) | copy-start | bytes 196612
  462.1 152.5 %copy-start.7 = (bf16[64,4,128]{2,1,0:T(4,128)(2,1)S(1)}, bf16[64,4,128]{2,1,0:T(4,128)(2,1)}, u32[]{:S(2)}) copy-start(bf16[64,4,128]{2,1,0:T(4,128)(2,1)} %reshape.109) | copy-start | bytes 196612
Sparse Core Ops, SparseCore 0:
  10.6 53.7 all-gather.3
  66.9 50.5 all-gather.5
  123.5 250.0 all-reduce.2
  375.9 76.1 all-gather.7
  617.9 248.6 all-reduce.4
where the time goes:
time: 876 us
  waiting for transfers between devices  674 us (77%)
  blocking collectives  150 us (17%)
  matrix products  16.3 us (2%)
  between operations  14.2 us (2%)
  other arithmetic  11.4 us (1%)
  local copies, waits for them, and re-layouts  9.33 us (1%)
    psum x1, waiting for transfers between devices, per_device(): lax.psum((block_part[1] * rescale, block_part[2] * spread(rescale)), ('ou...  247 us
    psum x1, waiting for transfers between devices, broadcast(): return lax.psum(block, axis)  247 us
    all_gather x1, waiting for transfers between devices, per_device(): lax.all_gather(w_query, 'inner', axis=0, tiled=True)  76.8 us
    pmax x1, blocking collectives, per_device(): highest = lax.pmax(block_part[0], ('outer', 'inner'))  76 us
    psum x1, blocking collectives, per_device(): lax.psum((block_part[1] * rescale, block_part[2] * spread(rescale)), ('ou...  74.4 us
    all_gather x1, waiting for transfers between devices, per_device(): lax.all_gather(w_key, 'inner', axis=0, tiled=True)  51.5 us
    all_gather x1, waiting for transfers between devices, per_device(): lax.all_gather(value_weight, 'inner', axis=0, tiled=True)  49.9 us
  transfers between devices with their start and end apart: 5, of which 5 were waited for; matrix products, arithmetic and copies ran while one was open for 2% of the time, Pallas kernels for 0%

commit v1 on v0

--- a/solution.py
+++ b/solution.py
@@ -115,7 +115,7 @@
     highest = lax.pmax(block_part[0], ("outer", "inner"))
     rescale = jnp.exp(block_part[0] - highest)
     summed_parts = lax.psum(
-        (block_part[1] * rescale, block_part[2] * spread(rescale)), ("outer", "inner")
+        lax.psum((block_part[1] * rescale, block_part[2] * spread(rescale)), "outer"), "inner"
     )
     merged = (highest, summed_parts[0], summed_parts[1])
     query_places = jnp.arange(query_count, dtype=jnp.int32)

time: 876 us -> 743 us (0.85)
  waiting for transfers between devices: 674 us -> 541 us
    psum x1 -> x2, waiting for transfers between devices: 247 us -> 111 us  [the longest x1 111 us: per_device(): lax.psum(lax.psum((block_part[1] * rescale, block_part[2] * spread(rescal...]
    psum x1 -> x2, blocking collectives: 74.4 us -> 75.4 us  [the longest x1 58.9 us: per_device(): lax.psum(lax.psum((block_part[1] * rescale, block_part[2] * spread(rescal...]
  transfers between devices with their start and end apart: 5 -> 6, of which waited for: 5 -> 5; matrix products, arithmetic and copies ran while one was open for 2% -> 2% of each run, Pallas kernels for 0% -> 0%
where the time goes in v1:
time: 743 us; the launch traced here: 741 us
  waiting for transfers between devices  541 us (73%)
  blocking collectives  151 us (20%)
  matrix products  16.4 us (2%)
  between operations  14.5 us (2%)
  other arithmetic  11.5 us (2%)
    psum x1, waiting for transfers between devices, broadcast(): return lax.psum(block, axis)  249 us
    psum x1, waiting for transfers between devices, per_device(): lax.psum(lax.psum((block_part[1] * rescale, block_part[2] * spread(rescal...  111 us
    all_gather x1, waiting for transfers between devices, per_device(): lax.all_gather(w_query, 'inner', axis=0, tiled=True)  77.4 us
    pmax x1, blocking collectives, per_device(): highest = lax.pmax(block_part[0], ('outer', 'inner'))  76 us
    psum x1, blocking collectives, per_device(): lax.psum(lax.psum((block_part[1] * rescale, block_part[2] * spread(rescal...  58.9 us
    all_gather x1, waiting for transfers between devices, per_device(): lax.all_gather(w_key, 'inner', axis=0, tiled=True)  51.5 us
    all_gather x1, waiting for transfers between devices, per_device(): lax.all_gather(value_weight, 'inner', axis=0, tiled=True)  49.9 us
    psum x1, blocking collectives, per_device(): lax.psum((block_part[1] * rescale, block_part[2] * spread(rescale)), 'out...  16.5 us
  transfers between devices with their start and end apart: 6, of which 5 were waited for; matrix products, arithmetic and copies ran while one was open for 2% of the time, Pallas kernels for 0%

profile of v1, /device:TPU:2, one launch (start us, length us, event | category | flops | bytes accessed | tf_op | source)
XLA Modules:
  0.0 740.8 jit_solution(17120468076888115843)
XLA Ops:
  7.2 0.0 all-gather.4.cloned.1.call-start
  7.2 0.7 all-gather.4.cloned.1.call-update
  7.9 0.0 all-gather.6.cloned.1.call-start
  8.0 0.7 all-gather.6.cloned.1.call-update
  8.7 0.0 all-reduce.4.cloned.1.call-start
  8.7 1.2 fusion.9
  10.0 1.5 fusion
  11.5 0.9 fusion.11
  12.5 0.3 fusion.2
  12.8 51.5 %all-gather.4.cloned.1.call-done = bf16[4096,512]{1,0:T(8,128)(2,1)} async-done(((bf16[128,512]{1,0:T(8,128)(2,1)}), bf16[4096,512]{1,0:T(8,128)(2,1)}) %all-gather.4.cloned.1.call-update) | async-done | bytes 4194320 | tf_op jit(solution)/shard_map/all_gather | solution.py:86
  64.3 3.2 convolution_convert_fusion.2
  67.6 49.9 %all-gather.6.cloned.1.call-done = bf16[4096,512]{1,0:T(8,128)(2,1)} async-done(((bf16[128,512]{1,0:T(8,128)(2,1)}), bf16[4096,512]{1,0:T(8,128)(2,1)}) %all-gather.6.cloned.1.call-update) | async-done | bytes 4194320 | tf_op jit(solution)/shard_map/all_gather | solution.py:87
  117.5 3.2 convolution_convert_fusion.1
  120.7 0.7 maximum_select_fusion
  121.4 0.0 all-reduce.4.cloned.1.call-update
  121.4 0.0 all-gather.8.cloned.1.call-start
  121.5 0.5 all-gather.8.cloned.1.call-update
  122.0 0.0 all-reduce.6.cloned.1.call-start
  122.1 0.6 fusion.52
  122.7 0.7 compare_and_fusion
  123.3 0.6 iota_compare_fusion.2
  124.0 0.1 fusion.37
  124.1 0.1 pad_add_fusion
  124.3 0.1 copy.28
  124.5 249.0 %all-reduce.4.cloned.1.call-done = bf16[2,128,512]{2,1,0:T(8,128)(2,1)} async-done(((bf16[2,128,512]{2,1,0:T(8,128)(2,1)}), bf16[2,128,512]{2,1,0:T(8,128)(2,1)}) %all-reduce.4.cloned.1.call-update) | async-done | bytes 262160 | tf_op jit(solution)/shard_map/psum | solution.py:14
  373.5 1.0 fusion.49
  374.6 0.1 copy.56
  374.7 77.4 %all-gather.8.cloned.1.call-done = bf16[4096,2048]{1,0:T(8,128)(2,1)} async-done(((bf16[128,2048]{1,0:T(8,128)(2,1)}), bf16[4096,2048]{1,0:T(8,128)(2,1)}) %all-gather.8.cloned.1.call-update) | async-done | bytes 16777232 | tf_op jit(solution)/shard_map/all_gather | solution.py:85
  452.2 7.7 %convolution_convert_fusion = bf16[192,2048]{1,0:T(8,128)(2,1)S(1)} fusion(bf16[4096,2048]{1,0:T(8,128)(2,1)} %all-gather.8.cloned.1.call-done, bf16[64,4096]{1,0:T(8,128)(2,1)S(1)} %fusion.11, bf16[128,4096]{1,0:T(8,128)(2,1)S(1)} %fusion.2), kind=kOutput, calls=%fused_computation.2 | convolution fusion | flops 3224764416 | bytes 19136512 | tf_op jit(solution)/shard_map/dot_general | solution.py:80
  459.9 0.4 reshape.98
  460.3 0.2 reshape.102
  460.5 0.4 fusion.54
  460.9 76.0 %pmax.7 = f32[16,64]{1,0:T(8,128)S(1)} all-reduce(f32[16,64]{1,0:T(8,128)S(1)} %bitcast.97), channel_id=1, replica_groups=mesh['outer'=8,'inner'=32] {'outer','inner'}, use_global_device_ids=true, to_apply=%region_6.7 | all-reduce | flops 1024 | bytes 8192 | tf_op jit(solution)/shard_map/pmax | solution.py:115
  536.9 0.4 fusion.19
  537.3 0.3 convolution_bitcast_fusion.1
  537.6 0.3 copy.38
  538.0 0.2 reshape.103
  538.2 0.1 copy.39
  538.3 0.2 broadcast_in_dim.71
  538.5 1.0 bitcast_multiply_fusion.2
  539.5 0.0 all-reduce.8.cloned.1.call-start
  539.6 0.5 fusion.53
  540.1 0.3 fusion.3
  540.4 0.5 fusion.12
  540.9 0.4 fusion.55
  541.3 0.1 fusion.21
  541.4 0.3 copy.34
  541.8 0.1 copy.33
  541.9 16.5 %psum.38 = f32[16,64]{1,0:T(8,128)S(1)} all-reduce(f32[16,64]{1,0:T(8,128)S(1)} %get-tuple-element.13), channel_id=1, replica_groups=mesh['outer'=8,'inner'=32] {'outer'}, use_global_device_ids=true, to_apply=%region_11.12 | all-reduce | flops 1024 | bytes 8192 | tf_op jit(solution)/shard_map/psum | solution.py:118
  558.4 58.9 %psum.39 = f32[16,64]{1,0:T(8,128)S(1)} all-reduce(f32[16,64]{1,0:T(8,128)S(1)} %psum.38), channel_id=1, replica_groups=mesh['outer'=8,'inner'=32] {'inner'}, use_global_device_ids=true, to_apply=%region_12.13 | all-reduce | flops 1024 | bytes 8192 | tf_op jit(solution)/shard_map/psum | solution.py:117
  617.3 0.1 copy.47
  617.4 0.3 convolution_bitcast_fusion
  617.7 0.3 copy.45
  618.0 0.2 reshape.110
  618.2 0.1 copy.46
  618.3 0.1 copy.42
  618.4 0.0 all-reduce.8.cloned.1.call-update
  618.4 0.3 broadcast_in_dim.68
  618.8 1.2 fusion.14
  619.9 111.2 %all-reduce.8.cloned.1.call-done = f32[64,2048]{1,0:T(8,128)} async-done(((f32[64,2048]{1,0:T(8,128)}), f32[64,2048]{1,0:T(8,128)}) %all-reduce.8.cloned.1.call-update) | async-done | bytes 524304 | tf_op jit(solution)/shard_map/psum | solution.py:117
  731.1 0.2 broadcast_in_dim.76
  731.3 0.2 broadcast_in_dim.75
  731.5 0.2 broadcast_in_dim.74
  731.7 2.2 fusion.16
  (29 shorter events, 0.4 us)
Async XLA Ops:
  7.2 4.4 copy-start.1
  7.2 5.3 copy-start
  7.2 5.3 copy-start.2
  7.2 57.1 %all-gather.4.cloned.1.call-start = ((), (), s32[]{:S(2)}) async-start(), calls=%async_computation | async-start | bytes 4325376 | tf_op jit(solution)/shard_map/all_gather | solution.py:86
  7.9 109.5 %all-gather.6.cloned.1.call-start = ((), (), s32[]{:S(2)}) async-start(), calls=%async_computation.1 | async-start | bytes 4325376 | tf_op jit(solution)/shard_map/all_gather | solution.py:87
  8.7 364.9 %all-reduce.4.cloned.1.call-start = ((), (), s32[]{:S(2)}) async-start(), calls=%async_computation.2 | async-start | bytes 524288 | tf_op jit(solution)/shard_map/psum | solution.py:14
  67.6 54.5 %copy-start.3 = (s32[256]{0:T(256)S(1)}, s32[256]{0:T(256)}, u32[]{:S(2)}) copy-start(s32[256]{0:T(256)} %param.13) | copy-start | bytes 3076
  121.4 330.7 %all-gather.8.cloned.1.call-start = ((), (), s32[]{:S(2)}) async-start(), calls=%async_computation.3 | async-start | bytes 17301504 | tf_op jit(solution)/shard_map/all_gather | solution.py:85
  122.0 496.4 %all-reduce.6.cloned.1.call-start = ((), (), s32[]{:S(2)}) async-start(), calls=%async_computation.4 | async-start | bytes 1048576 | tf_op jit(solution)/shard_map/psum | solution.py:118
  539.5 191.5 %all-reduce.8.cloned.1.call-start = ((), (), s32[]{:S(2)}) async-start(), calls=%async_computation.5 | async-start | bytes 1048576 | tf_op jit(solution)/shard_map/psum | solution.py:117
Sparse Core Ops, SparseCore 0:
  10.6 53.7 all-gather.3
  66.9 50.5 all-gather.5
  123.5 250.0 all-reduce.3
  376.0 76.1 all-gather.7
  539.7 70.6 all-reduce.5
  618.6 112.4 all-reduce.7
